TPU v7x, 512 devices: a whole 4x8x8 slice. The times are simulated.
512 devices in a mesh: dp: 16 (over z_hi, y), row: 8 (over x, core), col: 4 (over z_lo).
Axes of the slice: x: 4, y: 8, z: 8 (z_hi: 2, z_lo: 4; z = z_hi * 4 + z_lo), core: 2. Of those that a mesh axis runs over, the one named last changes fastest.
Arguments:
- inputs: bfloat16 [16, 512, 4, 1536], P('dp', 'col', None, 'row'), may hold values from -12 to 12
- gain: bfloat16 [4, 1536], P(None, 'row'), may hold values from 0.099609375 to 1.8984375
- weight: bfloat16 [6144, 6144], P('col', 'row'), may hold values from -0.078125 to 0.078125
- cotangent: bfloat16 [16, 512, 6144], P('dp', 'col', 'row'), may hold values from -3 to 3
Outputs:
- outputs: bfloat16 [16, 512, 6144], P('dp', 'col', 'row')
- input_grad: bfloat16 [16, 512, 4, 1536], P('dp', 'col', None, 'row')
- gain_grad: float32 [4, 1536], P(None, 'row')
- weight_grad: float32 [4, 1536, 6144], P('col', 'dp', 'row')
All inputs are finite; a program needn't handle non-finite values.
Results may differ from a plain program's by a relative error of at most 0.014.
Values may be sent and summed in bfloat16 or wider, within the bound.
A program may use at most 64 MiB of HBM per device.

v0:
```python
import jax
import jax.numpy as jnp
from jax import lax
from jax.sharding import PartitionSpec as P

D = 6144


EPS = 1e-05


def body(inputs, gain, weight, cotangent):
    token_rows = inputs.shape[1]
    blocks = inputs.shape[2]
    share = inputs.shape[3]
    local_in = inputs[0].astype(jnp.float32)
    gain_local = gain.astype(jnp.float32)
    totals = lax.psum(
        (jnp.sum(local_in, axis=(1, 2)), jnp.sum(local_in * local_in, axis=(1, 2))), "row"
    )
    mean = totals[0] / D
    variance = totals[1] / D - mean * mean
    inv_std = lax.rsqrt(variance + EPS)[:, None, None]
    normed = (local_in - mean[:, None, None]) * inv_std
    hidden_part = (normed * gain_local).astype(jnp.bfloat16)
    hidden = lax.all_gather(hidden_part, "row", axis=2, tiled=True)
    hidden = hidden.reshape(token_rows, D)
    cot_local = cotangent[0]
    weight_full = lax.all_gather(weight, "col", axis=0, tiled=True)
    outputs = jnp.dot(hidden, weight_full, preferred_element_type=jnp.float32).astype(jnp.bfloat16)
    cot_panel = lax.all_gather(cot_local, "col", axis=0, tiled=True)
    token_panel = lax.all_to_all(hidden, "col", split_axis=1, concat_axis=0, tiled=True)
    per_row = weight_full.reshape(blocks, lax.axis_size("row"), share, weight.shape[1])
    product = jnp.einsum("te,arje->tarj", cot_local, per_row, preferred_element_type=jnp.float32)
    back = lax.psum_scatter(
        product.astype(jnp.bfloat16), "row", scatter_dimension=2, tiled=True
    ).astype(jnp.float32)[:, :, 0, :]
    scaled = back * gain_local
    back_totals = lax.psum(
        (jnp.sum(scaled, axis=(1, 2)), jnp.sum(scaled * normed, axis=(1, 2))), "row"
    )
    first = (back_totals[0] / D)[:, None, None]
    second = (back_totals[1] / D)[:, None, None]
    input_grad = (inv_std * (scaled - first - normed * second)).astype(jnp.bfloat16)[None]
    groups = lax.axis_size("dp")
    gain_grad = lax.psum(jnp.sum(back * normed, axis=0), ("dp", "col")) / groups
    weight_grad = (
        lax.psum_scatter(
            lax.dot_general(
                token_panel, cot_panel, (((0,), (0,)), ((), ())), preferred_element_type=jnp.float32
            ).astype(jnp.bfloat16),
            "dp",
            scatter_dimension=0,
            tiled=True,
        ).astype(jnp.float32)
        / groups
    )
    return (outputs[None], input_grad, gain_grad, weight_grad[None])


def solution(mesh):
    return jax.shard_map(
        body,
        mesh=mesh,
        in_specs=(
            P("dp", "col", None, "row"),
            P(None, "row"),
            P("col", "row"),
            P("dp", "col", "row"),
        ),
        out_specs=(
            P("dp", "col", "row"),
            P("dp", "col", None, "row"),
            P(None, "row"),
            P("col", "dp", "row"),
        ),
        check_vma=False,
    )
```

profile of v0, /device:TPU:2, one launch (start us, length us, event | category | flops | bytes accessed | tf_op | source)
XLA Modules:
  0.0 609.2 jit_solution(10136297201713199577)
XLA Ops:
  7.2 0.0 copy-start.2
  7.2 0.0 all-gather.6.cloned.1.call-start
  7.2 0.7 all-gather.6.cloned.1.call-update
  7.9 0.0 all-reduce.5.cloned.1.call-start
  8.0 180.1 %all-gather.6.cloned.1.call-done = bf16[6144,768]{1,0:T(8,128)(2,1)} async-done(((bf16[1536,768]{1,0:T(8,128)(2,1)}), bf16[6144,768]{1,0:T(8,128)(2,1)}) %all-gather.6.cloned.1.call-update) | async-done | bytes 9437200 | tf_op jit(solution)/shard_map/all_gather | solution.py:29
  188.0 0.0 copy-done.2
  188.0 7.5 %convolution_convert_fusion.1 = bf16[128,4,8,192]{0,3,2,1:T(8,128)(2,1)} fusion(bf16[4,8,192,768]{3,2,1,0:T(8,128)(2,1)} %bitcast.85, bf16[1,128,768]{2,1,0:T(8,128)(2,1)S(1)} %copy-done.2), kind=kOutput, calls=%fused_computation.1 | convolution fusion | flops 1208745984 | bytes 11206656 | tf_op jit(solution)/shard_map/te,arje->tarj/dot_general | solution.py:34
  195.5 0.0 copy-start.3
  195.5 0.0 copy-start.1
  195.5 0.0 all-reduce.5.cloned.1.call-update
  195.5 0.0 all-gather.4.cloned.1.call-start
  195.6 0.6 copy-done.3
  196.2 1.3 dynamic-slice
  197.4 0.0 copy-done.1
  197.4 0.1 convert_reduce_fusion
  197.6 0.1 fusion.18
  197.7 11.5 %all-reduce.2 = (f32[128]{0:T(128)S(1)}, f32[128]{0:T(128)S(1)}) all-reduce(f32[128]{0:T(128)S(1)} %fusion.18, f32[128]{0:T(128)S(1)} %convert_reduce_fusion), channel_id=1, replica_groups=mesh['dp'=16,'row'=8,'col'=4] {'row'}, use_global_device_ids=true, to_apply=%region_3.0 | all-reduce | flops 256 | bytes 2048 | tf_op jit(solution)/shard_map/psum | solution.py:18
  209.1 58.4 %all-reduce.5.cloned.1.call-done = bf16[128,4,8,192]{0,3,2,1:T(8,128)(2,1)} async-done(((bf16[128,4,8,192]{0,3,2,1:T(8,128)(2,1)}), bf16[128,4,8,192]{0,3,2,1:T(8,128)(2,1)}) %all-reduce.5.cloned.1.call-update) | async-done | bytes 1572880
  267.5 3.0 fusion.9
  270.5 0.0 all-gather.4.cloned.1.call-update
  270.5 30.1 %all-gather.4.cloned.1.call-done = bf16[128,4,1536]{0,2,1:T(8,128)(2,1)} async-done(((bf16[128,4,192]{0,2,1:T(8,128)(2,1)}), bf16[128,4,1536]{0,2,1:T(8,128)(2,1)}) %all-gather.4.cloned.1.call-update) | async-done | bytes 1572880 | tf_op jit(solution)/shard_map/all_gather | solution.py:26
  300.6 5.1 all-to-all-start
  305.7 0.0 reduce-scatter.5.cloned.1.call-start
  305.7 51.5 %all-gather = bf16[1,512,768]{2,1,0:T(8,128)(2,1)} all-gather(bf16[1,128,768]{2,1,0:T(8,128)(2,1)S(1)} %copy-done.2), channel_id=2, replica_groups=mesh['dp'=16,'row'=8,'col'=4] {'col'}, dimensions={1}, use_global_device_ids=true | all-gather | bytes 983040 | tf_op jit(solution)/shard_map/all_gather | solution.py:31
  357.3 0.0 all-to-all-done
  357.3 0.7 copy.13
  358.0 4.0 convolution_convert_fusion
  361.9 0.0 copy-start.4
  361.9 0.0 copy-start.5
  361.9 0.0 copy-start
  361.9 0.0 reduce-scatter.5.cloned.1.call-update
  362.0 0.6 copy-done.4
  362.6 0.0 copy-done.5
  362.6 11.0 %all-reduce.1 = (f32[128]{0:T(128)S(1)}, f32[128]{0:T(128)S(1)}) all-reduce(f32[128]{0:T(128)S(1)} %copy-done.4, f32[128]{0:T(128)S(1)} %copy-done.5), channel_id=1, replica_groups=mesh['dp'=16,'row'=8,'col'=4] {'row'}, use_global_device_ids=true, to_apply=%region_8.0 | all-reduce | flops 256 | bytes 2048 | tf_op jit(solution)/shard_map/psum | solution.py:39
  373.6 145.1 %psum.39 = f32[4,192]{1,0:T(4,128)S(1)} all-reduce(f32[4,192]{1,0:T(4,128)S(1)} %get-tuple-element.8), channel_id=1, replica_groups=mesh['dp'=16,'row'=8,'col'=4] {'dp','col'}, use_global_device_ids=true, to_apply=%region_10.0 | all-reduce | flops 768 | bytes 6144 | tf_op jit(solution)/shard_map/psum | solution.py:46
  518.7 0.6 broadcast_multiply_fusion
  519.3 2.4 fusion.14
  521.7 0.0 copy-done
  521.7 5.8 fusion
  527.6 73.5 %reduce-scatter.5.cloned.1.call-done = bf16[96,768]{1,0:T(8,128)(2,1)} async-done(((bf16[1536,768]{1,0:T(8,128)(2,1)}), bf16[96,768]{1,0:T(8,128)(2,1)}) %reduce-scatter.5.cloned.1.call-update) | async-done | bytes 147472 | tf_op jit(solution)/shard_map/reduce_scatter | solution.py:48
  601.0 1.6 multiply_bitcast_fusion
  (3 shorter events, 0.0 us)
Async XLA Ops:
  7.2 180.9 %copy-start.2 = (bf16[1,128,768]{2,1,0:T(8,128)(2,1)S(1)}, bf16[1,128,768]{2,1,0:T(8,128)(2,1)}, u32[]{:S(2)}) copy-start(bf16[1,128,768]{2,1,0:T(8,128)(2,1)} %param.7) | copy-start | bytes 589828
  7.2 180.8 %all-gather.6.cloned.1.call-start = ((), (), s32[]{:S(2)}) async-start(), calls=%async_computation.3 | async-start | bytes 11796480 | tf_op jit(solution)/shard_map/all_gather | solution.py:29
  7.9 259.6 %all-reduce.5.cloned.1.call-start = ((), (), s32[]{:S(2)}) async-start(), calls=%async_computation.5 | async-start | bytes 3145728
  195.5 0.7 copy-start.3
  195.5 1.9 copy-start.1
  195.5 105.1 %all-gather.4.cloned.1.call-start = ((), (), s32[]{:S(2)}) async-start(), calls=%async_computation.2 | async-start | bytes 1769472 | tf_op jit(solution)/shard_map/all_gather | solution.py:26
  300.6 56.6 %all-to-all-start = ((bf16[128,4,1536]{0,2,1:T(8,128)(2,1)}), bf16[128,4,1536]{0,2,1:T(8,128)(2,1)S(1)}, u32[]{:S(2)}, u32[]{:S(2)}) async-start(bf16[128,4,1536]{0,2,1:T(8,128)(2,1)} %all-gather.4.cloned.1.call-done), calls=%async_computation | async-start | bytes 3145728 | tf_op jit(solution)/shard_map/all_to_all | solution.py:32
  305.7 295.3 %reduce-scatter.5.cloned.1.call-start = ((), (), s32[]{:S(2)}) async-start(), calls=%async_computation.4 | async-start | bytes 2506752 | tf_op jit(solution)/shard_map/reduce_scatter | solution.py:48
  361.9 0.7 copy-start.4
  361.9 0.7 copy-start.5
  361.9 159.8 %copy-start = (bf16[128,4,1536]{0,2,1:T(8,128)(2,1)S(1)}, bf16[128,4,1536]{0,2,1:T(8,128)(2,1)}, u32[]{:S(2)}) copy-start(bf16[128,4,1536]{0,2,1:T(8,128)(2,1)} %all-gather.4.cloned.1.call-done) | copy-start | bytes 4718596
Sparse Core Ops, SparseCore 0:
  10.1 177.8 all-gather.5
  195.6 71.8 all-reduce.4
  270.7 29.9 all-gather.3
  362.1 238.9 reduce-scatter.4
where the time goes:
time: 610 us; the launch traced here: 609 us
  waiting for transfers between devices  343 us (56%)
  blocking collectives  219 us (36%)
  matrix products  17.3 us (3%)
  between operations  13.8 us (2%)
  other arithmetic  7.91 us (1%)
    all_gather x1, waiting for transfers between devices, body(): weight_full = lax.all_gather(weight, 'col', axis=0, tiled=True)  180 us
    psum x1, blocking collectives, body(): gain_grad = lax.psum(jnp.sum(back * normed, axis=0), ('dp', 'col')) / groups  145 us
    reduce_scatter x1, waiting for transfers between devices, body(): lax.psum_scatter(lax.dot_general(token_panel, cot_panel, (((0,), (0,)), (...  73.5 us
    unnamed x5, waiting for transfers between devices  59.1 us
    all_gather x1, blocking collectives, body(): cot_panel = lax.all_gather(cot_local, 'col', axis=0, tiled=True)  51.5 us
    all_gather x1, waiting for transfers between devices, body(): hidden = lax.all_gather(hidden_part, 'row', axis=2, tiled=True)  30.1 us
  transfers between devices with their start and end apart: 5, of which 4 were waited for; matrix products, arithmetic and copies ran while one was open for 2% of the time, Pallas kernels for 0%

commit v1 on v0

v1 whole, which is shorter than its diff:
```python
import functools

import jax
import jax.numpy as jnp
from jax import lax
from jax.experimental import pallas as pl
from jax.experimental.pallas import tpu as pltpu
from jax.sharding import PartitionSpec as P

EPS = 1e-05
F32 = jnp.float32
BF16 = jnp.bfloat16
YS = 8
XS = 4
COPIES = 96


def al(value, to):
    return pl.multiple_of(value, to)


def kernel(
    x_ref, g_ref, w_ref, cot_ref,
    out_ref, ig_ref, gg_ref, wg_ref,
    stat, statr, normed, hid, gcol, panel, cotp, bsend, sibr,
    f1s, f1r, f2s, f2r, gs, bl, hst, hstr, osend, orecv, ofull,
    prod, rs, rr, zs, zr, gcb, gyb, gzs, gzr, ssem, rsem,
):
    blocks, share, tokens = x_ref.shape
    wide = cot_ref.shape[1]
    n_row, n_col, n_dp = lax.axis_size("row"), lax.axis_size("col"), lax.axis_size("dp")
    part = n_row * share
    width = n_row * blocks * share
    piece = part // n_dp
    half = wide // 2
    pair = 2 * tokens

    dp, row, col = lax.axis_index("dp"), lax.axis_index("row"), lax.axis_index("col")
    zh, y = dp // YS, dp % YS
    x, core = row // 2, row % 2
    cols = [col, col + 1 - 2 * (col % 2), (col + 2) % n_col, n_col - 1 - col]

    def at_row(r):
        return {"row": r}

    def at_x(step):
        return {"row": ((x + step + XS) % XS) * 2 + core}

    def at_col(c):
        return {"col": c}

    def at_y(step):
        return {"dp": zh * YS + (y + step + YS) % YS}

    sibling = {"row": x * 2 + 1 - core}
    partner = {"dp": (dp + YS) % n_dp}

    started = []

    def send(src, dst, device):
        index = len(started)
        copy = pltpu.make_async_remote_copy(
            src_ref=src,
            dst_ref=dst,
            send_sem=ssem.at[index],
            recv_sem=rsem.at[index],
            device_id=device,
            device_id_type=pl.DeviceIdType.MESH,
        )
        copy.start()
        started.append(copy)
        return copy

    barrier = pltpu.get_barrier_semaphore()
    peers = [at_row((row + k) % n_row) for k in range(1, n_row)]
    peers += [at_col(cols[k]) for k in range(1, n_col)]
    peers += [at_y(k) for k in range(1, YS)]
    peers += [partner]
    for peer in peers:
        pl.semaphore_signal(barrier, inc=1, device_id=peer, device_id_type=pl.DeviceIdType.MESH)

    values = x_ref[...].astype(F32)
    stat[0:1, :] = jnp.sum(values, axis=(0, 1)).reshape(1, tokens)
    stat[1:2, :] = jnp.sum(values * values, axis=(0, 1)).reshape(1, tokens)
    gcol[...] = jnp.transpose(jnp.broadcast_to(g_ref[...], (tokens, blocks * share)))
    cotp[pl.ds(al(col * tokens, tokens), tokens), :] = cot_ref[...]
    pl.semaphore_wait(barrier, len(peers))

    own_rows = pl.ds(al(col * tokens, tokens), tokens)
    stats = [send(stat, statr.at[k], at_row((row + k) % n_row)) for k in range(1, n_row)]
    cots = {1: send(cot_ref, cotp.at[own_rows, :], at_col(cols[1]))}

    total = stat[...]
    for k in range(1, n_row):
        stats[k - 1].wait_recv()
        total = total + statr[k]
    mean = total[0:1, :] / width
    variance = total[1:2, :] / width - mean * mean
    inv_std = lax.rsqrt(variance + EPS)
    flat = x_ref[...].astype(F32).reshape(blocks * share, tokens)
    norm = (flat - mean) * inv_std
    normed[...] = norm
    hid[...] = (norm * gcol[...]).astype(BF16).reshape(blocks, share, tokens)

    mine = pl.ds(al(row * share, share), share)
    own_lanes = pl.ds(al(col * tokens, tokens), tokens)
    moves = {k: send(hid.at[cols[k]], panel.at[mine, own_lanes], at_col(cols[k])) for k in (1, 3, 2)}
    panel[mine, own_lanes] = hid[col]
    for k in (3, 2):
        cots[k] = send(cot_ref, cotp.at[own_rows, :], at_col(cols[k]))

    def back_pair(p):
        lanes = pl.ds(al(p * pair, pair), pair)
        rhs_rows = pl.ds(al(p * pair, pair), pair)
        step = part // 2

        @pl.loop(0, 2)
        def _(i):
            rows = pl.ds(al(i * step, step), step)
            bsend[rows, lanes] = lax.dot_general(
                w_ref[rows, :], cotp[rhs_rows, :], (((1,), (1,)), ((), ())), preferred_element_type=F32
            ).astype(BF16)

        return [
            send(
                bsend.at[pl.ds(al((2 * xd + 1 - core) * share, share), share), lanes],
                sibr.at[xd, :, lanes],
                sibling,
            )
            for xd in range(XS)
        ]

    cots[1].wait_recv()
    sibs = back_pair(col // 2)

    for k in (1, 3, 2):
        moves[k].wait_recv()

    def block_of(step):
        return pl.ds(al((((x + step + XS) % XS) * 2 + core) * share, share), share)

    right = send(panel.at[mine, :], panel.at[mine, :], at_x(1))
    left = send(panel.at[mine, :], panel.at[mine, :], at_x(-1))
    gathers = [send(panel.at[mine, :], panel.at[mine, :], sibling)]
    low, high = pl.ds(0, pair), pl.ds(pair, pair)
    right.wait_recv()
    relay_right = send(panel.at[block_of(-1), low], panel.at[block_of(-1), low], at_x(1))
    gathers.append(send(panel.at[block_of(-1), :], panel.at[block_of(-1), :], sibling))
    left.wait_recv()
    relay_left = send(panel.at[block_of(1), high], panel.at[block_of(1), high], at_x(-1))
    gathers.append(send(panel.at[block_of(1), :], panel.at[block_of(1), :], sibling))
    relay_right.wait_recv()
    relay_left.wait_recv()
    gathers.append(send(panel.at[block_of(2), :], panel.at[block_of(2), :], sibling))
    for k in (3, 2):
        cots[k].wait_recv()
    for copy in gathers:
        copy.wait_recv()

    def grad_rows(targets):
        return jnp.concatenate(
            [panel[pl.ds(al((sub * YS + t) * piece, piece), piece), :] for sub, t in targets], axis=0
        )

    def product(targets):
        prod[0 : len(targets) * piece, :] = jnp.dot(
            grad_rows(targets), cotp[...], preferred_element_type=F32
        )

    ring = {}
    sides = (1, -1)

    def ring_start():
        opposite = (y + YS // 2) % YS
        product([(0, opposite), (1, opposite)])
        for h in range(2):
            for d in range(2):
                rs[d, h, 0, d] = prod[d * piece : (d + 1) * piece, h * half : (h + 1) * half].astype(BF16)
        for h in range(2):
            for d in range(2):
                ring[d, h, 0] = send(rs.at[d, h, 0, d], rr.at[d, h, 0, d], at_y(sides[d]))

    def ring_product(s):
        forward, backward = (y + YS // 2 - s) % YS, (y + YS // 2 + s) % YS
        product([(0, forward), (1, forward), (0, backward), (1, backward)])

    def ring_step(s):
        for h in range(2):
            for d in range(2):
                ring[d, h, s - 1].wait_recv()
                for sub in range(2):
                    at = (2 * d + sub) * piece
                    value = prod[at : at + piece, h * half : (h + 1) * half]
                    if s > 1 or sub == d:
                        value = value + rr[d, h, s - 1, sub].astype(F32)
                    rs[d, h, s, sub] = value.astype(BF16)
                ring[d, h, s] = send(rs.at[d, h, s], rr.at[d, h, s], at_y(sides[d]))

    last = YS // 2 - 1
    across = []

    def ring_end():
        for h in range(2):
            lanes = slice(h * half, (h + 1) * half)
            for d in range(2):
                ring[d, h, last].wait_recv()
            there = prod[piece : 2 * piece, lanes]
            there = there + rr[0, h, last, 1 - zh].astype(F32) + rr[1, h, last, 1 - zh].astype(F32)
            zs[h] = there.astype(BF16)
            across.append(send(zs.at[h], zr.at[h], partner))
            here = prod[0:piece, lanes]
            wg_ref[:, lanes] = here + rr[0, h, last, zh].astype(F32) + rr[1, h, last, zh].astype(F32)

    def out_pair(p):
        lhs = jnp.transpose(panel[:, pl.ds(al(p * pair, pair), pair)])
        ofull[...] = jnp.dot(lhs, w_ref[...], preferred_element_type=F32)
        osend[2 * p] = ofull[0:tokens, :].astype(BF16)
        osend[2 * p + 1] = ofull[tokens:pair, :].astype(BF16)

    def partial(xd):
        rows = pl.ds(al((2 * xd + core) * share, share), share)
        return bsend[rows, :].astype(F32) + sibr[xd].astype(F32)

    ring_start()
    ring_product(1)
    sibs += back_pair(1 - col // 2)
    ring_step(1)
    ring_product(2)
    out_pair(1 - col // 2)
    outs = {k: send(osend.at[cols[k]], orecv.at[k], at_col(cols[k])) for k in (3, 2)}
    ring_step(2)
    ring_product(3)
    for copy in sibs:
        copy.wait_recv()
    far = partial((x + 2) % XS)
    f1s[0] = far[:, 0:pair].astype(BF16)
    f1s[1] = far[:, pair : 2 * pair].astype(BF16)
    first_hop = [send(f1s.at[d], f1r.at[d], at_x(sides[d])) for d in range(2)]
    ring_step(3)
    product([(zh, y), (1 - zh, y)])
    out_pair(col // 2)
    outs[1] = send(osend.at[cols[1]], orecv.at[1], at_col(cols[1]))
    second_hop = []
    for d in range(2):
        near = partial((x + sides[d] + XS) % XS)
        first_hop[d].wait_recv()
        for i in range(2):
            value = near[:, i * pair : (i + 1) * pair]
            if i == d:
                value = value + f1r[d].astype(F32)
            f2s[d, :, i * pair : (i + 1) * pair] = value.astype(BF16)
        second_hop.append(send(f2s.at[d], f2r.at[d], at_x(sides[d])))
    ring_end()

    back = partial(x)
    for d in range(2):
        second_hop[d].wait_recv()
        back = back + f2r[d].astype(F32)
    for c in range(blocks):
        gs[c] = back[:, c * tokens : (c + 1) * tokens].astype(BF16)
    turns = [send(gs.at[cols[k]], bl.at[col], at_col(cols[k])) for k in (1, 2, 3)]
    bl[col] = gs[col]
    result = ofull[pl.ds(al((col % 2) * tokens, tokens), tokens), :]
    for k in (3, 2, 1):
        outs[k].wait_recv()
        result = result + orecv[k].astype(F32)
    out_ref[...] = result.astype(BF16)

    for copy in turns:
        copy.wait_recv()
    back = bl[...].astype(F32).reshape(blocks * share, tokens)
    scaled = back * gcol[...]
    hst[0:1, :] = jnp.sum(scaled, axis=0, keepdims=True)
    hst[1:2, :] = jnp.sum(scaled * normed[...], axis=0, keepdims=True)
    means = [send(hst, hstr.at[k], at_row((row + k) % n_row)) for k in range(1, n_row)]
    gcb[col] = jnp.sum(jnp.transpose(back * normed[...]), axis=0, keepdims=True)
    gain_cols = [send(gcb.at[col], gcb.at[col], at_col(cols[k])) for k in range(1, n_col)]

    sums = hst[...]
    for k in range(1, n_row):
        means[k - 1].wait_recv()
        sums = sums + hstr[k]
    first = sums[0:1, :] / width
    second = sums[1:2, :] / width
    grad = inv_std * (scaled - first - normed[...] * second)
    ig_ref[...] = grad.astype(BF16).reshape(blocks, share, tokens)

    for copy in gain_cols:
        copy.wait_recv()
    gyb[y] = gcb[0] + gcb[1] + gcb[2] + gcb[3]
    gain_ys = [send(gyb.at[y], gyb.at[y], at_y(k)) for k in range(1, YS)]
    for h in range(2):
        across[h].wait_recv()
        lanes = slice(h * half, (h + 1) * half)
        wg_ref[:, lanes] = (wg_ref[:, lanes] + zr[h].astype(F32)) / n_dp
    for copy in gain_ys:
        copy.wait_recv()
    group = gyb[0]
    for i in range(1, YS):
        group = group + gyb[i]
    gzs[...] = group
    gain_z = send(gzs, gzr, partner)
    gain_z.wait_recv()
    gg_ref[...] = (gzs[...] + gzr[...]) / n_dp
    for copy in started:
        copy.wait_send()


def body(inputs, gain, weight, cotangent):
    tokens, blocks, share = inputs.shape[1:]
    part, wide = weight.shape
    n_dp, n_row, n_col = lax.axis_size("dp"), lax.axis_size("row"), lax.axis_size("col")
    piece = part // n_dp
    half = wide // 2
    pair = 2 * tokens
    vmem = pl.BlockSpec(memory_space=pltpu.VMEM)
    outputs, input_grad, gain_grad, weight_grad = pl.pallas_call(
        kernel,
        out_shape=(
            jax.ShapeDtypeStruct((tokens, wide), BF16),
            jax.ShapeDtypeStruct((blocks, share, tokens), BF16),
            jax.ShapeDtypeStruct((1, blocks * share), F32),
            jax.ShapeDtypeStruct((piece, wide), F32),
        ),
        in_specs=[vmem] * 4,
        out_specs=(vmem,) * 4,
        scratch_shapes=[
            pltpu.VMEM((2, tokens), F32),
            pltpu.VMEM((n_row, 2, tokens), F32),
            pltpu.VMEM((blocks * share, tokens), F32),
            pltpu.VMEM((blocks, share, tokens), BF16),
            pltpu.VMEM((blocks * share, tokens), F32),
            pltpu.VMEM((part, n_col * tokens), BF16),
            pltpu.VMEM((n_col * tokens, wide), BF16),
            pltpu.VMEM((part, n_col * tokens), BF16),
            pltpu.VMEM((XS, share, n_col * tokens), BF16),
            pltpu.VMEM((2, share, pair), BF16),
            pltpu.VMEM((2, share, pair), BF16),
            pltpu.VMEM((2, share, 2 * pair), BF16),
            pltpu.VMEM((2, share, 2 * pair), BF16),
            pltpu.VMEM((n_col, share, tokens), BF16),
            pltpu.VMEM((n_col, share, tokens), BF16),
            pltpu.VMEM((2, tokens), F32),
            pltpu.VMEM((n_row, 2, tokens), F32),
            pltpu.VMEM((n_col, tokens, wide), BF16),
            pltpu.VMEM((n_col, tokens, wide), BF16),
            pltpu.VMEM((pair, wide), F32),
            pltpu.VMEM((4 * piece, wide), F32),
            pltpu.VMEM((2, 2, YS // 2, 2, piece, half), BF16),
            pltpu.VMEM((2, 2, YS // 2, 2, piece, half), BF16),
            pltpu.VMEM((2, piece, half), BF16),
            pltpu.VMEM((2, piece, half), BF16),
            pltpu.VMEM((n_col, 1, blocks * share), F32),
            pltpu.VMEM((YS, 1, blocks * share), F32),
            pltpu.VMEM((1, blocks * share), F32),
            pltpu.VMEM((1, blocks * share), F32),
            pltpu.SemaphoreType.DMA((COPIES,)),
            pltpu.SemaphoreType.DMA((COPIES,)),
        ],
        compiler_params=pltpu.CompilerParams(collective_id=0, has_side_effects=True),
    )(
        jnp.transpose(inputs[0], (1, 2, 0)),
        gain.astype(F32).reshape(1, blocks * share),
        weight,
        cotangent[0],
    )
    return (
        outputs[None],
        jnp.transpose(input_grad, (2, 0, 1))[None],
        gain_grad.reshape(blocks, share),
        weight_grad[None],
    )


def solution(mesh):
    return jax.shard_map(
        body,
        mesh=mesh,
        in_specs=(
            P("dp", "col", None, "row"),
            P(None, "row"),
            P("col", "row"),
            P("dp", "col", "row"),
        ),
        out_specs=(
            P("dp", "col", "row"),
            P("dp", "col", None, "row"),
            P(None, "row"),
            P("col", "dp", "row"),
        ),
        check_vma=False,
    )
```

time: 610 us -> 103 us (0.17)
  waiting for transfers between devices: 343 us -> 0 us
  blocking collectives: 219 us -> 0 us
  Pallas kernels: 0 us -> 94.3 us
  matrix products: 17.3 us -> 0 us
  between operations: 13.8 us -> 0.64 us
  other arithmetic: 7.91 us -> 0.68 us
    all_gather x2 -> x0, waiting for transfers between devices: 210 us -> none  [the longest x1 180 us: body(): weight_full = lax.all_gather(weight, 'col', axis=0, tiled=True)]
    psum x3 -> x0, blocking collectives: 168 us -> none  [the longest x1 145 us: body(): gain_grad = lax.psum(jnp.sum(back * normed, axis=0), ('dp', 'col')) / groups]
    pallas_call x0 -> x1, Pallas kernels: none -> 94.3 us  [body(): pl.pallas_call(kernel, out_shape=(jax.ShapeDtypeStruct((tokens, wide), BF...]
    reduce_scatter x1 -> x0, waiting for transfers between devices: 73.5 us -> none  [body(): lax.psum_scatter(lax.dot_general(token_panel, cot_panel, (((0,), (0,)), (...]
    unnamed x5 -> x0, waiting for transfers between devices: 59.1 us -> none
    all_gather x1 -> x0, blocking collectives: 51.5 us -> none  [body(): cot_panel = lax.all_gather(cot_local, 'col', axis=0, tiled=True)]
    dot_general x3 -> x0, matrix products: 17.3 us -> none  [the longest x1 7.47 us: body(): jnp.einsum('te,arje->tarj', cot_local, per_row, preferred_element_type=jn...]
  transfers between devices with their start and end apart: 5 -> 0, of which waited for: 4 -> 0; matrix products, arithmetic and copies ran while one was open for 2% -> 0% of each run, Pallas kernels for 0% -> 0%
where the time goes in v1:
time: 103 us
  Pallas kernels  94.3 us (92%)
  local copies, waits for them, and re-layouts  6.94 us (7%)
    pallas_call x1, Pallas kernels, body(): pl.pallas_call(kernel, out_shape=(jax.ShapeDtypeStruct((tokens, wide), BF...  94.3 us
    unnamed x3, local copies, waits for them, and re-layouts  4.92 us

profile of v1, /device:TPU:2, one launch (start us, length us, event | category | flops | bytes accessed | tf_op | source)
XLA Modules:
  0.0 102.6 jit_solution(16250917623299832920)
XLA Ops:
  0.6 1.3 %reshape.20.g_ref = f32[1,768]{1,0:T(1,128)} reshape(bf16[4,192]{1,0:T(4,128)(2,1)} %param.5) | data formatting | bytes 4608 | tf_op jit(solution)/shard_map/reshape | solution.py:363
  2.0 94.3 %shard_map.75 = (bf16[128,768]{1,0:T(8,128)(2,1)}, bf16[4,192,128]{2,1,0:T(8,128)(2,1)}, f32[1,768]{1,0:T(1,128)}, f32[96,768]{1,0:T(8,128)}) custom-call(bf16[4,192,128]{2,1,0:T(8,128)(2,1)} %bitcast.10, f32[1,768]{1,0:T(1,128)} %reshape.20.g_ref, bf16[1536,768]{1,0:T(8,128)(2,1)} %w_ref.1, bf16[128,768]{1,0:T(8,128)(2,1)} %bitcast.11), custom_call_target="tpu_custom_call" | custom-call | tf_op jit(solution)/shard_map/pallas_call | solution.py:317
  96.3 0.7 reduce
  97.0 0.7 reshape.18
  97.6 1.6 %copy.11 = bf16[1,128,768]{2,1,0:T(8,128)(2,1)} copy(bf16[1,128,768]{2,1,0:T(8,128)(2,1)} %bitcast.13) | data formatting | bytes 393216
  99.2 1.6 %copy.12 = bf16[1,128,4,192]{1,3,2,0:T(8,128)(2,1)} copy(bf16[1,128,4,192]{1,3,2,0:T(8,128)(2,1)} %bitcast.12) | data formatting | bytes 393216
  100.9 1.7 %copy.13 = f32[1,96,768]{2,1,0:T(8,128)} copy(f32[1,96,768]{2,1,0:T(8,128)} %bitcast.9) | data formatting | bytes 589824

commit v2 on v1

--- a/solution.py
+++ b/solution.py
@@ -20,11 +20,11 @@
 
 
 def kernel(
-    x_ref, g_ref, w_ref, cot_ref,
+    x_ref, g_ref, w_hbm, cot_ref,
     out_ref, ig_ref, gg_ref, wg_ref,
     stat, statr, normed, hid, gcol, panel, cotp, bsend, sibr,
-    f1s, f1r, f2s, f2r, gs, bl, hst, hstr, osend, orecv, ofull,
-    prod, rs, rr, zs, zr, gcb, gyb, gzs, gzr, ssem, rsem,
+    f1s, f1r, f2s, f2r, gs, bl, hst, hstr, osend, orecv, osum, ofull, w_ref,
+    prod, rs, rr, zs, zr, gcb, gyb, gzs, gzr, ssem, rsem, wsem,
 ):
     blocks, share, tokens = x_ref.shape
     wide = cot_ref.shape[1]
@@ -55,6 +55,8 @@
     sibling = {"row": x * 2 + 1 - core}
     partner = {"dp": (dp + YS) % n_dp}
 
+    weight_in = pltpu.make_async_copy(w_hbm, w_ref, wsem)
+    weight_in.start()
     started = []
 
     def send(src, dst, device):
@@ -82,13 +84,17 @@
     values = x_ref[...].astype(F32)
     stat[0:1, :] = jnp.sum(values, axis=(0, 1)).reshape(1, tokens)
     stat[1:2, :] = jnp.sum(values * values, axis=(0, 1)).reshape(1, tokens)
-    gcol[...] = jnp.transpose(jnp.broadcast_to(g_ref[...], (tokens, blocks * share)))
     cotp[pl.ds(al(col * tokens, tokens), tokens), :] = cot_ref[...]
     pl.semaphore_wait(barrier, len(peers))
 
     own_rows = pl.ds(al(col * tokens, tokens), tokens)
     stats = [send(stat, statr.at[k], at_row((row + k) % n_row)) for k in range(1, n_row)]
-    cots = {1: send(cot_ref, cotp.at[own_rows, :], at_col(cols[1]))}
+    cots = {k: send(cot_ref, cotp.at[own_rows, :], at_col(cols[k])) for k in (1, 3)}
+    gain = g_ref[...].astype(F32)
+    for a in range(blocks):
+        gcol[a * share : (a + 1) * share, :] = jnp.transpose(
+            jnp.broadcast_to(gain[a : a + 1, :], (tokens, share))
+        )
 
     total = stat[...]
     for k in range(1, n_row):
@@ -106,8 +112,9 @@
     own_lanes = pl.ds(al(col * tokens, tokens), tokens)
     moves = {k: send(hid.at[cols[k]], panel.at[mine, own_lanes], at_col(cols[k])) for k in (1, 3, 2)}
     panel[mine, own_lanes] = hid[col]
-    for k in (3, 2):
-        cots[k] = send(cot_ref, cotp.at[own_rows, :], at_col(cols[k]))
+    cots[3].wait_recv()
+    passed = pl.ds(al(cols[3] * tokens, tokens), tokens)
+    cots[2] = send(cotp.at[passed, :], cotp.at[passed, :], at_col(cols[1]))
 
     def back_pair(p):
         lanes = pl.ds(al(p * pair, pair), pair)
@@ -131,6 +138,7 @@
         ]
 
     cots[1].wait_recv()
+    weight_in.wait()
     sibs = back_pair(col // 2)
 
     for k in (1, 3, 2):
@@ -152,8 +160,19 @@
     relay_right.wait_recv()
     relay_left.wait_recv()
     gathers.append(send(panel.at[block_of(2), :], panel.at[block_of(2), :], sibling))
-    for k in (3, 2):
-        cots[k].wait_recv()
+    def partial(xd):
+        rows = pl.ds(al((2 * xd + core) * share, share), share)
+        return bsend[rows, :].astype(F32) + sibr[xd].astype(F32)
+
+    sides = (1, -1)
+    cots[2].wait_recv()
+    sibs += back_pair(1 - col // 2)
+    for copy in sibs:
+        copy.wait_recv()
+    far = partial((x + 2) % XS)
+    f1s[0] = far[:, 0:pair].astype(BF16)
+    f1s[1] = far[:, pair : 2 * pair].astype(BF16)
+    first_hop = [send(f1s.at[d], f1r.at[d], at_x(sides[d])) for d in range(2)]
     for copy in gathers:
         copy.wait_recv()
 
@@ -168,7 +187,6 @@
         )
 
     ring = {}
-    sides = (1, -1)
 
     def ring_start():
         opposite = (y + YS // 2) % YS
@@ -217,29 +235,8 @@
         osend[2 * p] = ofull[0:tokens, :].astype(BF16)
         osend[2 * p + 1] = ofull[tokens:pair, :].astype(BF16)
 
-    def partial(xd):
-        rows = pl.ds(al((2 * xd + core) * share, share), share)
-        return bsend[rows, :].astype(F32) + sibr[xd].astype(F32)
-
     ring_start()
     ring_product(1)
-    sibs += back_pair(1 - col // 2)
-    ring_step(1)
-    ring_product(2)
-    out_pair(1 - col // 2)
-    outs = {k: send(osend.at[cols[k]], orecv.at[k], at_col(cols[k])) for k in (3, 2)}
-    ring_step(2)
-    ring_product(3)
-    for copy in sibs:
-        copy.wait_recv()
-    far = partial((x + 2) % XS)
-    f1s[0] = far[:, 0:pair].astype(BF16)
-    f1s[1] = far[:, pair : 2 * pair].astype(BF16)
-    first_hop = [send(f1s.at[d], f1r.at[d], at_x(sides[d])) for d in range(2)]
-    ring_step(3)
-    product([(zh, y), (1 - zh, y)])
-    out_pair(col // 2)
-    outs[1] = send(osend.at[cols[1]], orecv.at[1], at_col(cols[1]))
     second_hop = []
     for d in range(2):
         near = partial((x + sides[d] + XS) % XS)
@@ -250,8 +247,10 @@
                 value = value + f1r[d].astype(F32)
             f2s[d, :, i * pair : (i + 1) * pair] = value.astype(BF16)
         second_hop.append(send(f2s.at[d], f2r.at[d], at_x(sides[d])))
-    ring_end()
-
+    ring_step(1)
+    out_pair(1 - col // 2)
+    handed = send(osend.at[cols[2]], orecv.at[0], at_col(cols[1]))
+    ring_product(2)
     back = partial(x)
     for d in range(2):
         second_hop[d].wait_recv()
@@ -260,11 +259,14 @@
         gs[c] = back[:, c * tokens : (c + 1) * tokens].astype(BF16)
     turns = [send(gs.at[cols[k]], bl.at[col], at_col(cols[k])) for k in (1, 2, 3)]
     bl[col] = gs[col]
-    result = ofull[pl.ds(al((col % 2) * tokens, tokens), tokens), :]
-    for k in (3, 2, 1):
-        outs[k].wait_recv()
-        result = result + orecv[k].astype(F32)
-    out_ref[...] = result.astype(BF16)
+    ring_step(2)
+    handed.wait_recv()
+    osum[...] = (osend[cols[3]].astype(F32) + orecv[0].astype(F32)).astype(BF16)
+    outs = [send(osum, orecv.at[1], at_col(cols[3]))]
+    out_pair(col // 2)
+    outs.append(send(osend.at[cols[1]], orecv.at[2], at_col(cols[1])))
+    ring_product(3)
+    ring_step(3)
 
     for copy in turns:
         copy.wait_recv()
@@ -275,6 +277,11 @@
     means = [send(hst, hstr.at[k], at_row((row + k) % n_row)) for k in range(1, n_row)]
     gcb[col] = jnp.sum(jnp.transpose(back * normed[...]), axis=0, keepdims=True)
     gain_cols = [send(gcb.at[col], gcb.at[col], at_col(cols[k])) for k in range(1, n_col)]
+    product([(zh, y), (1 - zh, y)])
+    for copy in gain_cols:
+        copy.wait_recv()
+    gzs[...] = gcb[0] + gcb[1] + gcb[2] + gcb[3]
+    gain_z = send(gzs, gzr, partner)
 
     sums = hst[...]
     for k in range(1, n_row):
@@ -282,26 +289,30 @@
         sums = sums + hstr[k]
     first = sums[0:1, :] / width
     second = sums[1:2, :] / width
-    grad = inv_std * (scaled - first - normed[...] * second)
+    grad = inv_std * (bl[...].astype(F32).reshape(blocks * share, tokens) * gcol[...] - first - normed[...] * second)
     ig_ref[...] = grad.astype(BF16).reshape(blocks, share, tokens)
-
-    for copy in gain_cols:
-        copy.wait_recv()
-    gyb[y] = gcb[0] + gcb[1] + gcb[2] + gcb[3]
+    ring_end()
+
+    gain_z.wait_recv()
+    gyb[y] = gzs[...] + gzr[...]
     gain_ys = [send(gyb.at[y], gyb.at[y], at_y(k)) for k in range(1, YS)]
-    for h in range(2):
-        across[h].wait_recv()
-        lanes = slice(h * half, (h + 1) * half)
-        wg_ref[:, lanes] = (wg_ref[:, lanes] + zr[h].astype(F32)) / n_dp
+    result = ofull[pl.ds(al((col % 2) * tokens, tokens), tokens), :]
+    for i in range(2):
+        outs[i].wait_recv()
+        result = result + orecv[1 + i].astype(F32)
+    out_ref[...] = result.astype(BF16)
     for copy in gain_ys:
         copy.wait_recv()
     group = gyb[0]
     for i in range(1, YS):
         group = group + gyb[i]
-    gzs[...] = group
-    gain_z = send(gzs, gzr, partner)
-    gain_z.wait_recv()
-    gg_ref[...] = (gzs[...] + gzr[...]) / n_dp
+    group = group / n_dp
+    for a in range(blocks):
+        gg_ref[a : a + 1, :] = group[:, a * share : (a + 1) * share]
+    for h in range(2):
+        across[h].wait_recv()
+        lanes = slice(h * half, (h + 1) * half)
+        wg_ref[:, lanes] = (wg_ref[:, lanes] + zr[h].astype(F32)) / n_dp
     for copy in started:
         copy.wait_send()
 
@@ -319,10 +330,10 @@
         out_shape=(
             jax.ShapeDtypeStruct((tokens, wide), BF16),
             jax.ShapeDtypeStruct((blocks, share, tokens), BF16),
-            jax.ShapeDtypeStruct((1, blocks * share), F32),
+            jax.ShapeDtypeStruct((blocks, share), F32),
             jax.ShapeDtypeStruct((piece, wide), F32),
         ),
-        in_specs=[vmem] * 4,
+        in_specs=[vmem, vmem, pl.BlockSpec(memory_space=pl.ANY), vmem],
         out_specs=(vmem,) * 4,
         scratch_shapes=[
             pltpu.VMEM((2, tokens), F32),
@@ -343,8 +354,10 @@
             pltpu.VMEM((2, tokens), F32),
             pltpu.VMEM((n_row, 2, tokens), F32),
             pltpu.VMEM((n_col, tokens, wide), BF16),
-            pltpu.VMEM((n_col, tokens, wide), BF16),
+            pltpu.VMEM((3, tokens, wide), BF16),
+            pltpu.VMEM((tokens, wide), BF16),
             pltpu.VMEM((pair, wide), F32),
+            pltpu.VMEM((part, wide), BF16),
             pltpu.VMEM((4 * piece, wide), F32),
             pltpu.VMEM((2, 2, YS // 2, 2, piece, half), BF16),
             pltpu.VMEM((2, 2, YS // 2, 2, piece, half), BF16),
@@ -356,18 +369,19 @@
             pltpu.VMEM((1, blocks * share), F32),
             pltpu.SemaphoreType.DMA((COPIES,)),
             pltpu.SemaphoreType.DMA((COPIES,)),
+            pltpu.SemaphoreType.DMA,
         ],
         compiler_params=pltpu.CompilerParams(collective_id=0, has_side_effects=True),
     )(
         jnp.transpose(inputs[0], (1, 2, 0)),
-        gain.astype(F32).reshape(1, blocks * share),
+        gain,
         weight,
         cotangent[0],
     )
     return (
         outputs[None],
         jnp.transpose(input_grad, (2, 0, 1))[None],
-        gain_grad.reshape(blocks, share),
+        gain_grad,
         weight_grad[None],
     )
 

time: 103 us -> 86.1 us (0.84)
  Pallas kernels: 94.3 us -> 79 us
    pallas_call x1, Pallas kernels: 94.3 us -> 79 us  [body(): pl.pallas_call(kernel, out_shape=(jax.ShapeDtypeStruct((tokens, wide), BF...]
    reshape x2 -> x0, local copies, waits for them, and re-layouts: 2.01 us -> none  [the longest x1 1.34 us: body(): gain.astype(F32).reshape(1, blocks * share)]
    unnamed x3 -> x4, local copies, waits for them, and re-layouts: 4.92 us -> 6.2 us
where the time goes in v2:
time: 86.1 us; the launch traced here: 85.8 us
  Pallas kernels  79 us (92%)
  local copies, waits for them, and re-layouts  6.2 us (7%)
    pallas_call x1, Pallas kernels, body(): pl.pallas_call(kernel, out_shape=(jax.ShapeDtypeStruct((tokens, wide), BF...  79 us
    unnamed x4, local copies, waits for them, and re-layouts  6.2 us

profile of v2, /device:TPU:2, one launch (start us, length us, event | category | flops | bytes accessed | tf_op | source)
XLA Modules:
  0.0 85.8 jit_solution(18009902549595543959)
XLA Ops:
  0.6 79.0 %shard_map.75 = (bf16[128,768]{1,0:T(8,128)(2,1)}, bf16[4,192,128]{2,1,0:T(8,128)(2,1)}, f32[4,192]{1,0:T(4,128)}, f32[96,768]{1,0:T(8,128)}) custom-call(bf16[4,192,128]{2,1,0:T(8,128)(2,1)} %bitcast.10, bf16[4,192]{1,0:T(4,128)(2,1)} %g_ref.1, bf16[1536,768]{1,0:T(8,128)(2,1)} %w_hbm.1, bf16[128,768]{1,0:T(8,128)(2,1)} %bitcast.11), custom_call_target="tpu_custom_call" | custom-call | tf_op jit(solution)/shard_map/pallas_call | solution.py:328
  79.6 1.6 %copy.12 = bf16[1,128,768]{2,1,0:T(8,128)(2,1)} copy(bf16[1,128,768]{2,1,0:T(8,128)(2,1)} %bitcast.13) | data formatting | bytes 393216
  81.2 1.6 %copy.13 = bf16[1,128,4,192]{1,3,2,0:T(8,128)(2,1)} copy(bf16[1,128,4,192]{1,3,2,0:T(8,128)(2,1)} %bitcast.12) | data formatting | bytes 393216
  82.8 1.3 %copy.14 = f32[4,192]{1,0:T(4,128)} copy(f32[4,192]{1,0:T(4,128)} %get-tuple-element.18) | data formatting | bytes 6144
  84.1 1.7 %copy.15 = f32[1,96,768]{2,1,0:T(8,128)} copy(f32[1,96,768]{2,1,0:T(8,128)} %bitcast.9) | data formatting | bytes 589824

commit v3 on v2

--- a/solution.py
+++ b/solution.py
@@ -89,7 +89,7 @@
 
     own_rows = pl.ds(al(col * tokens, tokens), tokens)
     stats = [send(stat, statr.at[k], at_row((row + k) % n_row)) for k in range(1, n_row)]
-    cots = {k: send(cot_ref, cotp.at[own_rows, :], at_col(cols[k])) for k in (1, 3)}
+    beside = send(cot_ref, cotp.at[own_rows, :], at_col(cols[1]))
     gain = g_ref[...].astype(F32)
     for a in range(blocks):
         gcol[a * share : (a + 1) * share, :] = jnp.transpose(
@@ -112,9 +112,11 @@
     own_lanes = pl.ds(al(col * tokens, tokens), tokens)
     moves = {k: send(hid.at[cols[k]], panel.at[mine, own_lanes], at_col(cols[k])) for k in (1, 3, 2)}
     panel[mine, own_lanes] = hid[col]
-    cots[3].wait_recv()
-    passed = pl.ds(al(cols[3] * tokens, tokens), tokens)
-    cots[2] = send(cotp.at[passed, :], cotp.at[passed, :], at_col(cols[1]))
+    few = tokens // 2
+    across_col = []
+    for i in range(2):
+        at = pl.ds(al(col * tokens + i * few, few), few)
+        across_col.append(send(cot_ref.at[pl.ds(i * few, few), :], cotp.at[at, :], at_col(cols[3])))
 
     def back_pair(p):
         lanes = pl.ds(al(p * pair, pair), pair)
@@ -137,7 +139,7 @@
             for xd in range(XS)
         ]
 
-    cots[1].wait_recv()
+    beside.wait_recv()
     weight_in.wait()
     sibs = back_pair(col // 2)
 
@@ -147,25 +149,36 @@
     def block_of(step):
         return pl.ds(al((((x + step + XS) % XS) * 2 + core) * share, share), share)
 
-    right = send(panel.at[mine, :], panel.at[mine, :], at_x(1))
-    left = send(panel.at[mine, :], panel.at[mine, :], at_x(-1))
+    low, high = pl.ds(0, pair), pl.ds(pair, pair)
+    right = [send(panel.at[mine, part_of], panel.at[mine, part_of], at_x(1)) for part_of in (low, high)]
+    left = [send(panel.at[mine, part_of], panel.at[mine, part_of], at_x(-1)) for part_of in (high, low)]
     gathers = [send(panel.at[mine, :], panel.at[mine, :], sibling)]
-    low, high = pl.ds(0, pair), pl.ds(pair, pair)
-    right.wait_recv()
-    relay_right = send(panel.at[block_of(-1), low], panel.at[block_of(-1), low], at_x(1))
+    passed = []
+    for i in range(2):
+        across_col[i].wait_recv()
+        at = pl.ds(al(cols[3] * tokens + i * few, few), few)
+        passed.append(send(cotp.at[at, :], cotp.at[at, :], at_col(cols[1])))
+        if i == 0:
+            right[0].wait_recv()
+            relay_right = send(panel.at[block_of(-1), low], panel.at[block_of(-1), low], at_x(1))
+            left[0].wait_recv()
+            relay_left = send(panel.at[block_of(1), high], panel.at[block_of(1), high], at_x(-1))
+    right[1].wait_recv()
     gathers.append(send(panel.at[block_of(-1), :], panel.at[block_of(-1), :], sibling))
-    left.wait_recv()
-    relay_left = send(panel.at[block_of(1), high], panel.at[block_of(1), high], at_x(-1))
+    left[1].wait_recv()
     gathers.append(send(panel.at[block_of(1), :], panel.at[block_of(1), :], sibling))
     relay_right.wait_recv()
+    gathers.append(send(panel.at[block_of(2), low], panel.at[block_of(2), low], sibling))
     relay_left.wait_recv()
-    gathers.append(send(panel.at[block_of(2), :], panel.at[block_of(2), :], sibling))
+    gathers.append(send(panel.at[block_of(2), high], panel.at[block_of(2), high], sibling))
+
     def partial(xd):
         rows = pl.ds(al((2 * xd + core) * share, share), share)
         return bsend[rows, :].astype(F32) + sibr[xd].astype(F32)
 
     sides = (1, -1)
-    cots[2].wait_recv()
+    for copy in passed:
+        copy.wait_recv()
     sibs += back_pair(1 - col // 2)
     for copy in sibs:
         copy.wait_recv()
@@ -317,6 +330,21 @@
         copy.wait_send()
 
 
+def hand_out(*refs):
+    n = (len(refs) - 2) // 3
+    sources, targets, held = refs[:n], refs[n : 2 * n], refs[2 * n : 3 * n]
+    isem, osem = refs[3 * n :]
+    reads = [pltpu.make_async_copy(sources[i], held[i], isem.at[i]) for i in range(n)]
+    writes = [pltpu.make_async_copy(held[i], targets[i], osem.at[i]) for i in range(n)]
+    for copy in reads:
+        copy.start()
+    for i in range(n):
+        reads[i].wait()
+        writes[i].start()
+    for copy in writes:
+        copy.wait()
+
+
 def body(inputs, gain, weight, cotangent):
     tokens, blocks, share = inputs.shape[1:]
     part, wide = weight.shape
@@ -325,7 +353,7 @@
     half = wide // 2
     pair = 2 * tokens
     vmem = pl.BlockSpec(memory_space=pltpu.VMEM)
-    outputs, input_grad, gain_grad, weight_grad = pl.pallas_call(
+    results = pl.pallas_call(
         kernel,
         out_shape=(
             jax.ShapeDtypeStruct((tokens, wide), BF16),
@@ -378,6 +406,15 @@
         weight,
         cotangent[0],
     )
+    anywhere = pl.BlockSpec(memory_space=pl.ANY)
+    outputs, input_grad, gain_grad, weight_grad = pl.pallas_call(
+        hand_out,
+        out_shape=tuple(jax.ShapeDtypeStruct(r.shape, r.dtype) for r in results),
+        in_specs=[anywhere] * len(results),
+        out_specs=(anywhere,) * len(results),
+        scratch_shapes=[pltpu.VMEM(r.shape, r.dtype) for r in results]
+        + [pltpu.SemaphoreType.DMA((len(results),)), pltpu.SemaphoreType.DMA((len(results),))],
+    )(*results)
     return (
         outputs[None],
         jnp.transpose(input_grad, (2, 0, 1))[None],

time: 86.1 us -> 81 us (0.941)
  the two profiles are of different devices: /device:TPU:2 before, /device:TPU:7 now
where the time goes in v3:
time: 81 us; the launch traced here: 80.8 us
  Pallas kernels  80.2 us (99%)
    pallas_call x1, Pallas kernels, body(): pl.pallas_call(kernel, out_shape=(jax.ShapeDtypeStruct((tokens, wide), BF...  78.2 us
    pallas_call x1, Pallas kernels, body(): pl.pallas_call(hand_out, out_shape=tuple((jax.ShapeDtypeStruct(r.shape, r...  1.95 us

profile of v3, /device:TPU:7, one launch (start us, length us, event | category | flops | bytes accessed | tf_op | source)
XLA Modules:
  0.0 80.8 jit_solution(11632433437433893917)
XLA Ops:
  0.6 78.2 %shard_map.75 = (bf16[128,768]{1,0:T(8,128)(2,1)}, bf16[4,192,128]{2,1,0:T(8,128)(2,1)}, f32[4,192]{1,0:T(4,128)}, f32[96,768]{1,0:T(8,128)}) custom-call(bf16[4,192,128]{2,1,0:T(8,128)(2,1)} %bitcast.9, bf16[4,192]{1,0:T(4,128)(2,1)} %g_ref.1, bf16[1536,768]{1,0:T(8,128)(2,1)} %w_hbm.1, bf16[128,768]{1,0:T(8,128)(2,1)} %bitcast.10), custom_call_target="tpu_custom_call" | custom-call | tf_op jit(solution)/shard_map/pallas_call | solution.py:356
  78.9 1.9 %shard_map.76 = (bf16[128,768]{1,0:T(8,128)(2,1)}, bf16[4,192,128]{2,1,0:T(8,128)(2,1)}, f32[4,192]{1,0:T(4,128)}, f32[96,768]{1,0:T(8,128)}) custom-call(bf16[128,768]{1,0:T(8,128)(2,1)} %get-tuple-element.12.refs_0_, bf16[4,192,128]{2,1,0:T(8,128)(2,1)} %get-tuple-element.13.refs_1_, f32[4,192]{1,0:T(4,128)} %get-tuple-element.14.refs_2_, ...), custom_call_target="tpu_custom_call" | custom-call | tf_op jit(solution)/shard_map/pallas_call | solution.py:410

commit v4 on v3

--- a/solution.py
+++ b/solution.py
@@ -179,13 +179,6 @@
     sides = (1, -1)
     for copy in passed:
         copy.wait_recv()
-    sibs += back_pair(1 - col // 2)
-    for copy in sibs:
-        copy.wait_recv()
-    far = partial((x + 2) % XS)
-    f1s[0] = far[:, 0:pair].astype(BF16)
-    f1s[1] = far[:, pair : 2 * pair].astype(BF16)
-    first_hop = [send(f1s.at[d], f1r.at[d], at_x(sides[d])) for d in range(2)]
     for copy in gathers:
         copy.wait_recv()
 
@@ -249,7 +242,17 @@
         osend[2 * p + 1] = ofull[tokens:pair, :].astype(BF16)
 
     ring_start()
+    sibs += back_pair(1 - col // 2)
     ring_product(1)
+    ring_step(1)
+    for copy in sibs:
+        copy.wait_recv()
+    far = partial((x + 2) % XS)
+    f1s[0] = far[:, 0:pair].astype(BF16)
+    f1s[1] = far[:, pair : 2 * pair].astype(BF16)
+    first_hop = [send(f1s.at[d], f1r.at[d], at_x(sides[d])) for d in range(2)]
+    out_pair(1 - col // 2)
+    handed = send(osend.at[cols[2]], orecv.at[0], at_col(cols[1]))
     second_hop = []
     for d in range(2):
         near = partial((x + sides[d] + XS) % XS)
@@ -260,10 +263,8 @@
                 value = value + f1r[d].astype(F32)
             f2s[d, :, i * pair : (i + 1) * pair] = value.astype(BF16)
         second_hop.append(send(f2s.at[d], f2r.at[d], at_x(sides[d])))
-    ring_step(1)
-    out_pair(1 - col // 2)
-    handed = send(osend.at[cols[2]], orecv.at[0], at_col(cols[1]))
     ring_product(2)
+    ring_step(2)
     back = partial(x)
     for d in range(2):
         second_hop[d].wait_recv()
@@ -272,7 +273,6 @@
         gs[c] = back[:, c * tokens : (c + 1) * tokens].astype(BF16)
     turns = [send(gs.at[cols[k]], bl.at[col], at_col(cols[k])) for k in (1, 2, 3)]
     bl[col] = gs[col]
-    ring_step(2)
     handed.wait_recv()
     osum[...] = (osend[cols[3]].astype(F32) + orecv[0].astype(F32)).astype(BF16)
     outs = [send(osum, orecv.at[1], at_col(cols[3]))]

time: 81 us -> 83.6 us (1.032)
  the two profiles are of different devices: /device:TPU:7 before, /device:TPU:64 now
where the time goes in v4:
time: 83.6 us; the launch traced here: 83.4 us
  Pallas kernels  82.8 us (99%)
    pallas_call x1, Pallas kernels, body(): pl.pallas_call(kernel, out_shape=(jax.ShapeDtypeStruct((tokens, wide), BF...  80.9 us
    pallas_call x1, Pallas kernels, body(): pl.pallas_call(hand_out, out_shape=tuple((jax.ShapeDtypeStruct(r.shape, r...  1.95 us

profile of v4, /device:TPU:64, one launch (start us, length us, event | category | flops | bytes accessed | tf_op | source)
XLA Modules:
  0.0 83.4 jit_solution(13334708330803826027)
XLA Ops:
  0.6 80.9 %shard_map.75 = (bf16[128,768]{1,0:T(8,128)(2,1)}, bf16[4,192,128]{2,1,0:T(8,128)(2,1)}, f32[4,192]{1,0:T(4,128)}, f32[96,768]{1,0:T(8,128)}) custom-call(bf16[4,192,128]{2,1,0:T(8,128)(2,1)} %bitcast.9, bf16[4,192]{1,0:T(4,128)(2,1)} %g_ref.1, bf16[1536,768]{1,0:T(8,128)(2,1)} %w_hbm.1, bf16[128,768]{1,0:T(8,128)(2,1)} %bitcast.10), custom_call_target="tpu_custom_call" | custom-call | tf_op jit(solution)/shard_map/pallas_call | solution.py:356
  81.5 1.9 %shard_map.76 = (bf16[128,768]{1,0:T(8,128)(2,1)}, bf16[4,192,128]{2,1,0:T(8,128)(2,1)}, f32[4,192]{1,0:T(4,128)}, f32[96,768]{1,0:T(8,128)}) custom-call(bf16[128,768]{1,0:T(8,128)(2,1)} %get-tuple-element.12.refs_0_, bf16[4,192,128]{2,1,0:T(8,128)(2,1)} %get-tuple-element.13.refs_1_, f32[4,192]{1,0:T(4,128)} %get-tuple-element.14.refs_2_, ...), custom_call_target="tpu_custom_call" | custom-call | tf_op jit(solution)/shard_map/pallas_call | solution.py:410
